TPU v7x, 32 devices: a whole 2x2x4 slice. The times are simulated.
32 devices in a mesh: row: 4 (over y, core), col: 8 (over z, x).
Axes of the slice: x: 2, y: 2, z: 4, core: 2. Of those that a mesh axis runs over, the one named last changes fastest.
Arguments:
- positions: float32 [512, 147], P(('row', 'col')), may hold values from -0.55 to 9.45, as said below
- coefficients: float32 [512, 147], P(('row', 'col')), may hold values from -6 to 6
- atom_pairs: int32 [2, 1176], replicated, may hold values from 0 to 48, as said below
- pair_scale: float32 [1176], replicated, may hold values from 0.5 to 2
Outputs:
- applied: float32 [512, 147], P(('row', 'col'))
Inputs may be any that keep to these rules, and one draw needn't show every extreme that they name: `atom_pairs`: every unordered pair of two different atoms stands in exactly one column, the smaller atom in row 0. `positions`: every two atoms of a geometry lie 0.6 or more apart; all geometries are displacements of one molecule.
All inputs are finite; a program needn't handle non-finite values.
Results may differ from a plain program's by a relative error of at most 0.0003.
Values sent between devices are 32-bit elements; how exact they have to be, the bound alone decides.
A program may use at most 64 MiB of HBM per device.

v0:
```python
import functools
import math

import jax
import jax.numpy as jnp
from jax import lax
from jax.experimental import pallas as pl
from jax.experimental.pallas import tpu as pltpu
from jax.sharding import PartitionSpec as P

length_scale = 2.0
decay_rate = math.sqrt(5.0) / length_scale
outer_factor = decay_rate * decay_rate / 3.0
radial_factor = decay_rate * decay_rate

LANES = 128
HALF = 64
TILE = 256
f32, bf16 = jnp.float32, jnp.bfloat16


def dot(a, b):
    return jnp.dot(a, b, preferred_element_type=f32)


def rounded(v):
    return v.astype(bf16).astype(f32)


def two_parts(v):
    hi = v.astype(bf16)
    return hi, (v - hi.astype(f32)).astype(bf16)


def operands(packed):
    hi = rounded(packed)
    rest = packed - hi
    mid = rounded(rest)
    low = pltpu.roll(rest - mid, HALF, 1)
    first = lax.broadcasted_iota(jnp.int32, packed.shape, 1) < HALF
    hi = hi.astype(bf16)
    for_spans = jnp.concatenate([hi, jnp.where(first, mid, low).astype(bf16)], axis=1)
    for_moves = jnp.concatenate([hi, jnp.where(first, low, mid).astype(bf16)], axis=1)
    return for_spans, for_moves


MESH = pl.DeviceIdType.MESH


def plan(row_count, col_count):
    cores = 2 if row_count % 2 == 0 else 1
    sides = 2 if col_count % 2 == 0 else 1
    nears = 2 if (col_count // sides) % 2 == 0 else 1
    fars, ys = col_count // sides // nears, row_count // cores
    summed = [(y, 0, n, x, 0) for y in range(ys) for n in range(nears) for x in range(sides)]
    shared = [(0, f, 0, 0, c) for f in range(fars) for c in range(cores)]
    summed.sort(key=lambda o: sum(v > 0 for v in o))
    shared.sort(key=lambda o: sum(v > 0 for v in o))
    return (ys, fars, nears, sides, cores), summed, shared


def kernel(
    row_count, col_count, per, atoms, width,
    pos_hbm, coef_hbm, pairs_hbm, scale_hbm, out_ref,
    pos_in, coef_in, pairs_in, scale_in, cols, rows, pairs, scale, table_s, table_m,
    row_s, row_x, row_w, row_t, hold_x, hold_u, partial, landed,
    local, send_col, recv_col, send_row, recv_row, send_sum, recv_sum,
):
    row = lax.axis_index("row")
    col = lax.axis_index("col")
    padded = table_s.shape[1]
    block = 3 * per
    sizes, summed, group = plan(row_count, col_count)
    wide_count, tall_count = len(summed), len(group)
    count = wide_count * per
    tall = tall_count * per
    ys, fars, nears, sides, cores = sizes
    here = (row // cores, col // (sides * nears), lax.rem(col // sides, nears), lax.rem(col, sides), lax.rem(row, cores))

    def peer(offset, sign):
        y, far, near, side, core = [
            lax.rem(at + (step if sign > 0 else size - step), size)
            for at, step, size in zip(here, offset, sizes)
        ]
        return (y * cores + core, (far * nears + near) * sides + side)

    loads = [
        pltpu.make_async_copy(src, dst, local.at[i])
        for i, (src, dst) in enumerate(
            [(pos_hbm, pos_in), (coef_hbm, coef_in), (pairs_hbm, pairs_in), (scale_hbm, scale_in)]
        )
    ]
    for load in loads:
        load.start()
    barrier = pltpu.get_barrier_semaphore()
    for offset in summed[1:] + group[1:]:
        pl.semaphore_signal(barrier, inc=1, device_id=peer(offset, 1), device_id_type=MESH)

    loads[0].wait()
    loads[1].wait()
    position, coefficient = pos_in[...], coef_in[...]
    gap = jnp.zeros((per, HALF - atoms), f32)
    for k in range(3):
        cut = slice(k * atoms, (k + 1) * atoms)
        packed = jnp.concatenate([position[:, cut], gap, coefficient[:, cut], gap], axis=1)
        cols[k * per : (k + 1) * per, :] = packed
        rows[k * per : (k + 1) * per, :] = packed

    pl.semaphore_wait(barrier, wide_count - 1 + tall_count - 1)
    spread = []
    for s in reversed(range(1, wide_count)):
        spread.append(
            pltpu.make_async_remote_copy(
                src_ref=cols.at[pl.ds(0, block)],
                dst_ref=cols.at[pl.ds(s * block, block)],
                send_sem=send_col.at[s],
                recv_sem=recv_col.at[s],
                device_id=peer(summed[s], -1),
                device_id_type=MESH,
            )
        )
    shared = []
    for k in range(1, tall_count):
        shared.append(
            pltpu.make_async_remote_copy(
                src_ref=rows.at[pl.ds(0, block)],
                dst_ref=rows.at[pl.ds(k * block, block)],
                send_sem=send_row.at[k],
                recv_sem=recv_row.at[k],
                device_id=peer(group[k], -1),
                device_id_type=MESH,
            )
        )
    for copy in spread + shared:
        copy.start()

    loads[2].wait()
    loads[3].wait()
    pairs[...] = jnp.full(pairs.shape, -1, jnp.int32)
    pairs[0:2, 0:width] = pairs_in[...]
    scale[...] = jnp.zeros(scale.shape, f32)
    scale[0:1, 0:width] = scale_in[...].reshape(1, width)
    ids = lax.broadcasted_iota(jnp.int32, (HALF, padded), 0)
    signs = (jnp.where(ids == pairs[0:1, :], 1.0, 0.0) - jnp.where(ids == pairs[1:2, :], 1.0, 0.0)).astype(bf16)
    blank = jnp.zeros((HALF, padded), bf16)
    for q in range(4):
        table_s[q * HALF : (q + 1) * HALF, :] = blank if q == 1 else signs
        table_m[q * HALF : (q + 1) * HALF, :] = blank if q == 0 else signs

    def spans_at(for_spans, geoms, t):
        cut = slice(t * TILE, (t + 1) * TILE)
        spans = dot(for_spans, table_s[:, cut])
        parts = spans.reshape(geoms, 3, per, TILE)
        square = parts[:, 0] * parts[:, 0] + parts[:, 1] * parts[:, 1] + parts[:, 2] * parts[:, 2]
        square = square.reshape(geoms * per, TILE)
        if (t + 1) * TILE > width:
            lane = lax.broadcasted_iota(jnp.int32, square.shape, 1)
            square = jnp.where(lane < width - t * TILE, square, 1.0)
        inverse = lax.rsqrt(square)
        features = scale[0:1, cut] * inverse
        return spans, features, features * inverse * inverse

    for copy in shared:
        copy.wait_recv()
    for_spans, _ = operands(rows[...])
    row_square = jnp.zeros((tall, 1), f32)
    for t in range(padded // TILE):
        cut = slice(t * TILE, (t + 1) * TILE)
        spans, features, weights = spans_at(for_spans, tall_count, t)
        row_s[:, cut] = spans
        row_x[:, cut] = features
        row_w[:, cut] = weights
        row_square += jnp.sum(features * features, axis=1, keepdims=True)
        hi = rounded(features)
        stacked = [hi, features - hi]
        if row_t.shape[1] > 2 * tall:
            stacked.append(jnp.zeros((row_t.shape[1] - 2 * tall, TILE), f32))
        row_t[cut, :] = jnp.concatenate(stacked, axis=0).T.astype(bf16)

    for copy in spread:
        copy.wait_recv()
    for_spans, for_moves = operands(cols[...])
    square = jnp.zeros((count, LANES), f32)
    mixed = jnp.zeros((count, LANES), f32)
    for t in range(padded // TILE):
        cut = slice(t * TILE, (t + 1) * TILE)
        spans, features, weights = spans_at(for_spans, wide_count, t)
        moves = dot(for_moves, table_m[:, cut]).reshape(wide_count, 3, per, TILE)
        spans = spans.reshape(wide_count, 3, per, TILE)
        inner = spans[:, 0] * moves[:, 0] + spans[:, 1] * moves[:, 1] + spans[:, 2] * moves[:, 2]
        tangents = -weights * inner.reshape(count, TILE)
        for part in range(TILE // LANES):
            x = features[:, part * LANES : (part + 1) * LANES]
            u = tangents[:, part * LANES : (part + 1) * LANES]
            square += x * x
            mixed += x * u
        hi, low = two_parts(features)
        hold_x[0:count, cut] = hi
        hold_x[count : 2 * count, cut] = low
        hi, low = two_parts(tangents)
        hold_u[0:count, cut] = hi
        hold_u[count : 2 * count, cut] = low

    turned = row_t[...]
    gram = dot(hold_x[...], turned)
    gram = (gram[0:count] + gram[count : 2 * count]).T
    gram = gram[0:tall] + gram[tall : 2 * tall]
    cross = dot(hold_u[...], turned)
    cross = (cross[0:count] + cross[count : 2 * count]).T
    cross = cross[0:tall] + cross[tall : 2 * tall]
    square = jnp.sum(square.T, axis=0, keepdims=True)
    mixed = jnp.sum(mixed.T, axis=0, keepdims=True)
    radius = jnp.sqrt(jnp.maximum(row_square + square - 2.0 * gram, 0.0))
    envelope = outer_factor * jnp.exp(-decay_rate * radius)
    direct = envelope * (1.0 + decay_rate * radius)
    bent = radial_factor * (envelope * (cross - mixed))
    bent_sum = jnp.sum(bent, axis=1, keepdims=True)

    def doubled(v):
        hi = rounded(v)
        both = jnp.concatenate([hi, v - hi], axis=0).astype(bf16)
        return jnp.concatenate([both, both], axis=1)

    direct, bent = doubled(direct), doubled(bent)
    result = jnp.zeros((2 * tall_count * block, HALF), f32)
    for t in range(padded // TILE):
        cut = slice(t * TILE, (t + 1) * TILE)
        grads = dot(direct, hold_u[:, cut]) + dot(bent, hold_x[:, cut])
        grads = grads[0:tall] + grads[tall : 2 * tall] - bent_sum * row_x[:, cut]
        pulled = -(row_w[:, cut] * grads).reshape(tall_count, 1, per, TILE)
        whole = (pulled * row_s[:, cut].reshape(tall_count, 3, per, TILE)).reshape(tall_count * block, TILE)
        hi, low = two_parts(whole)
        result += lax.dot_general(
            jnp.concatenate([hi, low], axis=0), table_s[0:HALF, cut], (((1,), (1,)), ((), ())),
            preferred_element_type=f32,
        )
    result = result[0 : tall_count * block] + result[tall_count * block :]

    sums = []
    for k in range(tall_count):
        r = [result[k * block + i * per : k * block + (i + 1) * per] for i in range(3)]
        partial[k, 0:per] = jnp.concatenate([r[0], r[1]], axis=1)
        partial[k, per:] = jnp.concatenate([r[2][0 : per // 2], r[2][per // 2 :]], axis=1)
        if k:
            sums.append(
                pltpu.make_async_remote_copy(
                    src_ref=partial.at[k],
                    dst_ref=landed.at[k],
                    send_sem=send_sum.at[k],
                    recv_sem=recv_sum.at[k],
                    device_id=peer(group[k], 1),
                    device_id_type=MESH,
                )
            )
    for copy in sums:
        copy.start()
    for copy in spread + shared:
        copy.wait_send()
    total = partial[0]
    for k, copy in enumerate(sums):
        copy.wait_recv()
        total += landed[k + 1]
    first, second, third = total[0:per, 0:atoms], total[0:per, HALF : HALF + atoms], total[per:]
    third = jnp.concatenate([third[:, 0:atoms], third[:, HALF : HALF + atoms]], axis=0)
    out_ref[...] = jnp.concatenate([first, second, third], axis=1)
    for copy in sums:
        copy.wait_send()


def on_device(positions, coefficients, atom_pairs, pair_scale):
    row_count = lax.axis_size("row")
    col_count = lax.axis_size("col")
    per = positions.shape[0]
    atoms = positions.shape[1] // 3
    width = atom_pairs.shape[1]
    padded = -(-width // TILE) * TILE
    _, summed, group = plan(row_count, col_count)
    count = len(summed) * per
    tall = len(group) * per
    anywhere = pl.BlockSpec(memory_space=pltpu.MemorySpace.HBM)
    return pl.pallas_call(
        functools.partial(kernel, row_count, col_count, per, atoms, width),
        out_shape=jax.ShapeDtypeStruct(positions.shape, f32),
        in_specs=[anywhere] * 4,
        out_specs=pl.BlockSpec(memory_space=pltpu.VMEM),
        scratch_shapes=[
            pltpu.VMEM(positions.shape, f32),
            pltpu.VMEM(coefficients.shape, f32),
            pltpu.VMEM(atom_pairs.shape, jnp.int32),
            pltpu.VMEM(pair_scale.shape, f32),
            pltpu.VMEM((3 * count, LANES), f32),
            pltpu.VMEM((3 * tall, LANES), f32),
            pltpu.VMEM((8, padded), jnp.int32),
            pltpu.VMEM((8, padded), f32),
            pltpu.VMEM((TILE, padded), bf16),
            pltpu.VMEM((TILE, padded), bf16),
            pltpu.VMEM((3 * tall, padded), f32),
            pltpu.VMEM((tall, padded), f32),
            pltpu.VMEM((tall, padded), f32),
            pltpu.VMEM((padded, -(-2 * tall // LANES) * LANES), bf16),
            pltpu.VMEM((2 * count, padded), bf16),
            pltpu.VMEM((2 * count, padded), bf16),
            pltpu.VMEM((len(group), 3 * per // 2, LANES), f32),
            pltpu.VMEM((len(group), 3 * per // 2, LANES), f32),
            pltpu.SemaphoreType.DMA((4,)),
            pltpu.SemaphoreType.DMA((len(summed),)),
            pltpu.SemaphoreType.DMA((len(summed),)),
            pltpu.SemaphoreType.DMA((len(group),)),
            pltpu.SemaphoreType.DMA((len(group),)),
            pltpu.SemaphoreType.DMA((len(group),)),
            pltpu.SemaphoreType.DMA((len(group),)),
        ],
        compiler_params=pltpu.CompilerParams(
            collective_id=0, has_side_effects=True, vmem_limit_bytes=60 * 1024 * 1024
        ),
    )(positions, coefficients, atom_pairs, pair_scale)


def solution(mesh):
    in_specs = (P(("row", "col"), None), P(("row", "col"), None), P(), P())
    out_specs = P(("row", "col"), None)
    return jax.shard_map(
        on_device, mesh=mesh, in_specs=in_specs, out_specs=out_specs, check_vma=False
    )
```

profile of v0, /device:TPU:0, one launch (start us, length us, event | category | flops | bytes accessed | tf_op | source)
XLA Modules:
  0.0 18.1 jit_solution(2685078277513537015)
XLA Ops:
  0.0 16.7 %shard_map.46 = f32[16,147]{1,0:T(8,128)} custom-call(f32[16,147]{1,0:T(8,128)} %pos_hbm.1, f32[16,147]{1,0:T(8,128)} %coef_hbm.1, s32[2,1176]{1,0:T(2,128)} %pairs_hbm.1, f32[1176]{0:T(1024)} %scale_hbm.1), custom_call_target="tpu_custom_call" | custom-call | tf_op jit(solution)/shard_map/pallas_call | solution.py:281
  16.7 1.3 %copy.6 = f32[16,147]{1,0:T(8,128)} copy(f32[16,147]{1,0:T(8,128)} %shard_map.46) | data formatting | bytes 18816
where the time goes:
time: 18.4 us; the launch traced here: 18.1 us
  Pallas kernels  16.7 us (91%)
  local copies, waits for them, and re-layouts  1.32 us (7%)
    pallas_call x1, Pallas kernels, on_device(): pl.pallas_call(functools.partial(kernel, row_count, col_count, per, atoms...  16.7 us
    unnamed x1, local copies, waits for them, and re-layouts  1.32 us

commit v1 on v0

--- a/solution.py
+++ b/solution.py
@@ -100,38 +100,40 @@
     loads[1].wait()
     position, coefficient = pos_in[...], coef_in[...]
     gap = jnp.zeros((per, HALF - atoms), f32)
+    part = per // 2
+    short = 3 * part
     for k in range(3):
         cut = slice(k * atoms, (k + 1) * atoms)
         packed = jnp.concatenate([position[:, cut], gap, coefficient[:, cut], gap], axis=1)
         cols[k * per : (k + 1) * per, :] = packed
-        rows[k * per : (k + 1) * per, :] = packed
+        rows[k * part : (k + 1) * part, :] = jnp.concatenate(
+            [position[0:part, cut], gap[0:part], position[part:, cut], gap[0:part]], axis=1
+        )
 
     pl.semaphore_wait(barrier, wide_count - 1 + tall_count - 1)
-    spread = []
-    for s in reversed(range(1, wide_count)):
-        spread.append(
-            pltpu.make_async_remote_copy(
-                src_ref=cols.at[pl.ds(0, block)],
-                dst_ref=cols.at[pl.ds(s * block, block)],
-                send_sem=send_col.at[s],
-                recv_sem=recv_col.at[s],
-                device_id=peer(summed[s], -1),
-                device_id_type=MESH,
-            )
+    spread = {}
+    for s in range(1, wide_count):
+        spread[s] = pltpu.make_async_remote_copy(
+            src_ref=cols.at[pl.ds(0, block)],
+            dst_ref=cols.at[pl.ds(s * block, block)],
+            send_sem=send_col.at[s],
+            recv_sem=recv_col.at[s],
+            device_id=peer(summed[s], -1),
+            device_id_type=MESH,
         )
     shared = []
     for k in range(1, tall_count):
         shared.append(
             pltpu.make_async_remote_copy(
-                src_ref=rows.at[pl.ds(0, block)],
-                dst_ref=rows.at[pl.ds(k * block, block)],
+                src_ref=rows.at[pl.ds(0, short)],
+                dst_ref=rows.at[pl.ds(k * short, short)],
                 send_sem=send_row.at[k],
                 recv_sem=recv_row.at[k],
                 device_id=peer(group[k], -1),
                 device_id_type=MESH,
             )
         )
-    for copy in spread + shared:
+    for copy in list(spread.values()) + shared:
         copy.start()
 
     loads[2].wait()
@@ -147,10 +149,8 @@
         table_s[q * HALF : (q + 1) * HALF, :] = blank if q == 1 else signs
         table_m[q * HALF : (q + 1) * HALF, :] = blank if q == 0 else signs
 
-    def spans_at(for_spans, geoms, t):
+    def terms(parts, geoms, t):
         cut = slice(t * TILE, (t + 1) * TILE)
-        spans = dot(for_spans, table_s[:, cut])
-        parts = spans.reshape(geoms, 3, per, TILE)
         square = parts[:, 0] * parts[:, 0] + parts[:, 1] * parts[:, 1] + parts[:, 2] * parts[:, 2]
         square = square.reshape(geoms * per, TILE)
         if (t + 1) * TILE > width:
@@ -158,16 +158,67 @@
             square = jnp.where(lane < width - t * TILE, square, 1.0)
         inverse = lax.rsqrt(square)
         features = scale[0:1, cut] * inverse
-        return spans, features, features * inverse * inverse
+        return features, features * inverse * inverse
+
+    def summed_terms(low, high):
+        many = high - low
+        size, base = many * per, 2 * low * per
+        for_spans, for_moves = operands(cols[low * block : high * block, :])
+        square = jnp.zeros((size, LANES), f32)
+        mixed = jnp.zeros((size, LANES), f32)
+        for t in range(padded // TILE):
+            cut = slice(t * TILE, (t + 1) * TILE)
+            spans = dot(for_spans, table_s[:, cut]).reshape(many, 3, per, TILE)
+            moves = dot(for_moves, table_m[:, cut]).reshape(many, 3, per, TILE)
+            features, weights = terms(spans, many, t)
+            inner = spans[:, 0] * moves[:, 0] + spans[:, 1] * moves[:, 1] + spans[:, 2] * moves[:, 2]
+            tangents = -weights * inner.reshape(size, TILE)
+            for lane in range(0, TILE, LANES):
+                x = features[:, lane : lane + LANES]
+                u = tangents[:, lane : lane + LANES]
+                square += x * x
+                mixed += x * u
+            for hold, value in ((hold_x, features), (hold_u, tangents)):
+                hi, rest = two_parts(value)
+                hold[base : base + size, cut] = hi
+                hold[base + size : base + 2 * size, cut] = rest
+        return jnp.sum(square.T, axis=0, keepdims=True), jnp.sum(mixed.T, axis=0, keepdims=True)
+
+    def doubled(v):
+        hi = rounded(v)
+        both = jnp.concatenate([hi, v - hi], axis=0).astype(bf16)
+        return [both, both]
+
+    def coupled(low, high, square, mixed):
+        size, base = (high - low) * per, 2 * low * per
+        turned = row_t[...]
+
+        def against(hold):
+            both = dot(hold[base : base + 2 * size, :], turned)
+            both = (both[0:size] + both[size : 2 * size]).T
+            return both[0:tall] + both[tall : 2 * tall]
+
+        radius = jnp.sqrt(jnp.maximum(row_square + square - 2.0 * against(hold_x), 0.0))
+        envelope = outer_factor * jnp.exp(-decay_rate * radius)
+        direct = envelope * (1.0 + decay_rate * radius)
+        bent = radial_factor * (envelope * (against(hold_u) - mixed))
+        return doubled(direct), doubled(bent), jnp.sum(bent, axis=1, keepdims=True)
+
+    half = (wide_count + 1) // 2
+    for s in range(1, half):
+        spread[s].wait_recv()
+    near_sums = summed_terms(0, half)
 
     for copy in shared:
         copy.wait_recv()
-    for_spans, _ = operands(rows[...])
+    lower, upper = operands(rows[...])
     row_square = jnp.zeros((tall, 1), f32)
     for t in range(padded // TILE):
         cut = slice(t * TILE, (t + 1) * TILE)
-        spans, features, weights = spans_at(for_spans, tall_count, t)
-        row_s[:, cut] = spans
+        halves = [dot(lower, table_s[:, cut]), dot(upper, table_m[:, cut])]
+        spans = jnp.concatenate([v.reshape(tall_count, 3, part, TILE) for v in halves], axis=2)
+        features, weights = terms(spans, tall_count, t)
+        row_s[:, cut] = spans.reshape(3 * tall, TILE)
         row_x[:, cut] = features
         row_w[:, cut] = weights
         row_square += jnp.sum(features * features, axis=1, keepdims=True)
@@ -177,51 +228,13 @@
             stacked.append(jnp.zeros((row_t.shape[1] - 2 * tall, TILE), f32))
         row_t[cut, :] = jnp.concatenate(stacked, axis=0).T.astype(bf16)
 
-    for copy in spread:
-        copy.wait_recv()
-    for_spans, for_moves = operands(cols[...])
-    square = jnp.zeros((count, LANES), f32)
-    mixed = jnp.zeros((count, LANES), f32)
-    for t in range(padded // TILE):
-        cut = slice(t * TILE, (t + 1) * TILE)
-        spans, features, weights = spans_at(for_spans, wide_count, t)
-        moves = dot(for_moves, table_m[:, cut]).reshape(wide_count, 3, per, TILE)
-        spans = spans.reshape(wide_count, 3, per, TILE)
-        inner = spans[:, 0] * moves[:, 0] + spans[:, 1] * moves[:, 1] + spans[:, 2] * moves[:, 2]
-        tangents = -weights * inner.reshape(count, TILE)
-        for part in range(TILE // LANES):
-            x = features[:, part * LANES : (part + 1) * LANES]
-            u = tangents[:, part * LANES : (part + 1) * LANES]
-            square += x * x
-            mixed += x * u
-        hi, low = two_parts(features)
-        hold_x[0:count, cut] = hi
-        hold_x[count : 2 * count, cut] = low
-        hi, low = two_parts(tangents)
-        hold_u[0:count, cut] = hi
-        hold_u[count : 2 * count, cut] = low
-
-    turned = row_t[...]
-    gram = dot(hold_x[...], turned)
-    gram = (gram[0:count] + gram[count : 2 * count]).T
-    gram = gram[0:tall] + gram[tall : 2 * tall]
-    cross = dot(hold_u[...], turned)
-    cross = (cross[0:count] + cross[count : 2 * count]).T
-    cross = cross[0:tall] + cross[tall : 2 * tall]
-    square = jnp.sum(square.T, axis=0, keepdims=True)
-    mixed = jnp.sum(mixed.T, axis=0, keepdims=True)
-    radius = jnp.sqrt(jnp.maximum(row_square + square - 2.0 * gram, 0.0))
-    envelope = outer_factor * jnp.exp(-decay_rate * radius)
-    direct = envelope * (1.0 + decay_rate * radius)
-    bent = radial_factor * (envelope * (cross - mixed))
-    bent_sum = jnp.sum(bent, axis=1, keepdims=True)
-
-    def doubled(v):
-        hi = rounded(v)
-        both = jnp.concatenate([hi, v - hi], axis=0).astype(bf16)
-        return jnp.concatenate([both, both], axis=1)
-
-    direct, bent = doubled(direct), doubled(bent)
+    direct, bent, bent_sum = coupled(0, half, *near_sums)
+    if half < wide_count:
+        for s in range(half, wide_count):
+            spread[s].wait_recv()
+        more = coupled(half, wide_count, *summed_terms(half, wide_count))
+        direct, bent, bent_sum = direct + more[0], bent + more[1], bent_sum + more[2]
+    direct, bent = jnp.concatenate(direct, axis=1), jnp.concatenate(bent, axis=1)
     result = jnp.zeros((2 * tall_count * block, HALF), f32)
     for t in range(padded // TILE):
         cut = slice(t * TILE, (t + 1) * TILE)
@@ -254,7 +267,7 @@
             )
     for copy in sums:
         copy.start()
-    for copy in spread + shared:
+    for copy in list(spread.values()) + shared:
         copy.wait_send()
     total = partial[0]
     for k, copy in enumerate(sums):
@@ -289,7 +302,7 @@
             pltpu.VMEM(atom_pairs.shape, jnp.int32),
             pltpu.VMEM(pair_scale.shape, f32),
             pltpu.VMEM((3 * count, LANES), f32),
-            pltpu.VMEM((3 * tall, LANES), f32),
+            pltpu.VMEM((3 * tall // 2, LANES), f32),
             pltpu.VMEM((8, padded), jnp.int32),
             pltpu.VMEM((8, padded), f32),
             pltpu.VMEM((TILE, padded), bf16),
@@ -311,9 +324,9 @@
             pltpu.SemaphoreType.DMA((len(group),)),
         ],
         compiler_params=pltpu.CompilerParams(
-            collective_id=0, has_side_effects=True, vmem_limit_bytes=60 * 1024 * 1024
+            collective_id=0, has_side_effects=True, vmem_limit_bytes=40 * 1024 * 1024
         ),
-    )(positions, coefficients, atom_pairs, pair_scale)
+    )(*[pltpu.with_memory_space_constraint(v, pltpu.MemorySpace.HBM) for v in (positions, coefficients, atom_pairs, pair_scale)])
 
 
 def solution(mesh):

time: 18.4 us -> 16.6 us (0.902)
  Pallas kernels: 16.7 us -> 15.7 us
  local copies, waits for them, and re-layouts: 1.32 us -> 0.61 us
    pallas_call x1, Pallas kernels: 16.7 us -> 15.7 us  [on_device(): pl.pallas_call(functools.partial(kernel, row_count, col_count, per, atoms...]
    unnamed x1, local copies, waits for them, and re-layouts: 1.32 us -> 0.61 us
where the time goes in v1:
time: 16.6 us; the launch traced here: 16.4 us
  Pallas kernels  15.7 us (95%)
  local copies, waits for them, and re-layouts  0.61 us (4%)
    pallas_call x1, Pallas kernels, on_device(): pl.pallas_call(functools.partial(kernel, row_count, col_count, per, atoms...  15.7 us
    unnamed x1, local copies, waits for them, and re-layouts  0.61 us

profile of v1, /device:TPU:0, one launch (start us, length us, event | category | flops | bytes accessed | tf_op | source)
XLA Modules:
  0.0 16.4 jit_solution(11893343904048789426)
XLA Ops:
  0.0 15.7 %shard_map.46 = f32[16,147]{1,0:T(8,128)S(1)} custom-call(f32[16,147]{1,0:T(8,128)} %pos_hbm.1, f32[16,147]{1,0:T(8,128)} %coef_hbm.1, s32[2,1176]{1,0:T(2,128)} %pairs_hbm.1, f32[1176]{0:T(1024)} %scale_hbm.1), custom_call_target="tpu_custom_call" | custom-call | tf_op jit(solution)/shard_map/pallas_call | solution.py:294
  15.8 0.6 %copy.6 = f32[16,147]{1,0:T(8,128)} copy(f32[16,147]{1,0:T(8,128)S(1)} %shard_map.46) | data formatting | bytes 18816
